TPU v7x, 128 devices: a whole 4x4x4 slice. The times are simulated.
128 devices in a mesh: seq: 16 (over x, y), head: 8 (over z, core).
Axes of the slice: x: 4, y: 4, z: 4, core: 2. Of those that a mesh axis runs over, the one named last changes fastest.
Arguments:
- query_rows: bfloat16 [65536, 2048], P(('seq', 'head')), may hold values from -6 to 6
- key_rows: bfloat16 [65536, 2048], P(('seq', 'head')), may hold values from -6 to 6
- value_rows: bfloat16 [65536, 2048], P(('seq', 'head')), may hold values from -6 to 6
- gate_rows: bfloat16 [65536, 2048], P(('seq', 'head')), may hold values from -6 to 6
- segment_ids: int32 [512], P('seq'), may hold values from 0 to 3, as said below
- decay_rates: float32 [16], replicated, may hold values from 7.6293946e-07 to 0.00030517578
- norm_gain: float32 [2048], replicated, may hold values from 0.25 to 1.75
- out_weight: bfloat16 [2048, 2048], P(('seq', 'head')), may hold values from -0.125 to 0.125
Outputs:
- mixed_out: bfloat16 [65536, 2048], P(('seq', 'head'))
Inputs may be any that keep to these rules, and one draw needn't show every extreme that they name: segment_ids never falls from one block to the next; every document number appears, each document spans 1 to 256 blocks and one spans exactly 256.
All inputs are finite; a program needn't handle non-finite values.
Results may differ from a plain program's by a relative error of at most 0.006.
Values may be sent and summed in bfloat16 or wider, within the bound.
A program may use at most 256 MiB of HBM per device.

v0:
```python
import jax
import jax.numpy as jnp
from jax import lax
from jax.sharding import Mesh
from jax.sharding import PartitionSpec as P

BLK = 128
SBLK = 512
HEAD = ("head_0", "head_1")
SEQ_HEAD = ("seq_0", "seq_1", "head_0", "head_1")
SEQ = ("seq_0", "seq_1")
three_pass = lax.Precision.HIGH


def neutral_like(array, identity):
    return jax.tree.map(
        lambda a, e: jnp.broadcast_to(jnp.asarray(e, a.dtype), a.shape), array, identity
    )


def prefix_by_axis(array, axes, combine, identity):
    before = start = neutral_like(array, identity)
    subtotal = array
    for axis in reversed(axes):
        count, index = (lax.axis_size(axis), lax.axis_index(axis))
        pieces = jax.tree.map(lambda part: lax.all_gather(part, axis), subtotal)
        inside, subtotal = (start, start)
        for k in range(count):
            passed = k < index
            subtotal = combine(subtotal, jax.tree.map(lambda part: part[k], pieces))
            inside = jax.tree.map(lambda new, old: jnp.where(passed, new, old), subtotal, inside)
        before = combine(inside, before)
    return before


def attend_local(queries, keys_here, values_here, tok_seg, rates_local):
    tok_count, head_count, head_width = queries.shape
    blocks = tok_count // SBLK
    positions = jnp.arange(SBLK, dtype=jnp.float32)
    offsets = positions[:, None] - positions[None, :]
    causal = offsets >= 0
    lagged = jnp.exp(-rates_local[:, None, None] * jnp.maximum(offsets, 0.0)[None])
    reach_base = jnp.exp(-rates_local[None, :] * (positions[:, None] + 1.0))
    keep_base = jnp.exp(-rates_local[None, :] * (SBLK - 1.0 - positions[:, None]))
    block_decay = jnp.exp(-rates_local * SBLK)

    def advance(carried, blocks_in):
        state_now, prev_seg = carried
        query_part, key_part, value_part, seg_part = blocks_in
        same_doc = (seg_part[:, None] == seg_part[None, :]) & causal
        scores = jnp.einsum(
            "ihd,jhd->hij", query_part, key_part, preferred_element_type=jnp.float32
        )
        weights = jnp.where(same_doc[None], scores * lagged, 0.0).astype(jnp.bfloat16)
        inner_part = jnp.einsum(
            "hij,jhd->ihd", weights, value_part, preferred_element_type=jnp.float32
        )
        reach_row = jnp.where((seg_part == prev_seg)[:, None], reach_base, 0.0)
        outer_part = reach_row[:, :, None] * jnp.einsum(
            "ihd,hde->ihe", query_part.astype(jnp.float32), state_now, precision=three_pass
        )
        last_seg = seg_part[-1]
        keep_row = jnp.where((seg_part == last_seg)[:, None], keep_base, 0.0)
        kept_keys = key_part.astype(jnp.float32) * keep_row[:, :, None]
        carry_keep = jnp.where(last_seg == prev_seg, block_decay, 0.0)
        new_state = carry_keep[:, None, None] * state_now + jnp.einsum(
            "jhd,jhe->hde", kept_keys, value_part.astype(jnp.float32), precision=three_pass
        )
        return ((new_state, last_seg), inner_part + outer_part)

    start = (
        jnp.zeros((head_count, head_width, head_width), jnp.float32),
        jnp.array(-1.0, jnp.float32),
    )
    shaped = (
        queries.reshape(blocks, SBLK, head_count, head_width),
        keys_here.reshape(blocks, SBLK, head_count, head_width),
        values_here.reshape(blocks, SBLK, head_count, head_width),
        tok_seg.reshape(blocks, SBLK),
    )
    finished, outputs = lax.scan(advance, start, shaped)
    return (outputs.reshape(tok_count, head_count, head_width), finished[0])


def add_carried(local_out, queries, tok_seg, rates_local, state_in, seg_in):
    positions = jnp.arange(queries.shape[0], dtype=jnp.float32)
    reach_row = jnp.where(
        (tok_seg == seg_in)[:, None],
        jnp.exp(-rates_local[None, :] * (positions[:, None] + 1.0)),
        0.0,
    )
    carried = jnp.einsum(
        "ihd,hde->ihe", queries.astype(jnp.float32), state_in, precision=three_pass
    )
    return (local_out + reach_row[:, :, None] * carried).astype(jnp.bfloat16)


def link_pieces(earlier, later):
    state_early, decay_early, first_early, last_early = earlier
    state_late, decay_late, first_late, last_late = later
    joined = (last_early == first_late) | (last_early < 0) | (first_late < 0)
    factor = jnp.where(joined, decay_late, 0.0)
    state_both = state_late + factor[:, None, None] * state_early
    decay_both = jnp.where(joined, decay_early * decay_late, 0.0)
    first_both = jnp.where(first_early < 0, first_late, first_early)
    last_both = jnp.where(last_late < 0, last_early, last_late)
    return (state_both, decay_both, first_both, last_both)


def summary_of(state_end, tok_seg, rates_local):
    tok_count = tok_seg.shape[0]
    whole_doc = jnp.where(tok_seg[0] == tok_seg[-1], jnp.exp(-rates_local * tok_count), 0.0)
    head_count = rates_local.shape[0]
    identity = (
        jnp.zeros_like(state_end),
        jnp.ones((head_count,), jnp.float32),
        -jnp.ones((1,), jnp.float32),
        -jnp.ones((1,), jnp.float32),
    )
    return ((state_end, whole_doc, tok_seg[:1], tok_seg[-1:]), identity)


def on_device(
    query_rows, key_rows, value_rows, gate_rows, segment_ids, decay_rates, norm_gain, out_weight
):
    tok_dev = query_rows.shape[0]
    head_total = decay_rates.shape[0]
    head_width = query_rows.shape[1] // head_total
    shaped = (
        query_rows.reshape(tok_dev, head_total, head_width),
        key_rows.reshape(tok_dev, head_total, head_width),
        value_rows.reshape(tok_dev, head_total, head_width),
    )
    blocks_dev = tok_dev // BLK
    own_ids = lax.dynamic_slice_in_dim(segment_ids, lax.axis_index(HEAD) * blocks_dev, blocks_dev)
    tok_seg = jnp.repeat(own_ids, BLK).astype(jnp.float32)
    queries, keys_here, values_here = shaped
    local_out, state_end = attend_local(queries, keys_here, values_here, tok_seg, decay_rates)
    summary, identity = summary_of(state_end, tok_seg, decay_rates)
    state_in, decay_in, first_in, last_in = prefix_by_axis(summary, SEQ_HEAD, link_pieces, identity)
    attention = add_carried(local_out, queries, tok_seg, decay_rates, state_in, last_in[0])
    widened = attention.astype(jnp.float32)
    inv_rms = lax.rsqrt(jnp.mean(widened * widened, axis=-1, keepdims=True) + 1e-06)
    normed = (widened * inv_rms).reshape(tok_dev, head_total * head_width)
    normed = (normed * norm_gain * jax.nn.silu(gate_rows.astype(jnp.float32))).astype(jnp.bfloat16)
    mixed_out = jnp.dot(
        normed,
        lax.all_gather(out_weight, SEQ_HEAD, axis=0, tiled=True),
        preferred_element_type=jnp.float32,
    )
    return mixed_out.astype(jnp.bfloat16)


def solution(mesh):
    split = Mesh(mesh.devices.reshape(4, 4, 4, 2), ("seq_0", "seq_1", "head_0", "head_1"))
    return jax.shard_map(
        on_device,
        mesh=split,
        in_specs=(
            P(SEQ_HEAD, None),
            P(SEQ_HEAD, None),
            P(SEQ_HEAD, None),
            P(SEQ_HEAD, None),
            P(SEQ),
            P(),
            P(),
            P(SEQ_HEAD, None),
        ),
        out_specs=P(SEQ_HEAD, None),
        check_vma=False,
    )
```

profile of v0, /device:TPU:1, one launch (start us, length us, event | category | flops | bytes accessed | tf_op | source)
XLA Modules:
  0.0 351.8 jit_solution(2318212796308319544)
XLA Ops:
  13.9 3.5 %all-reduce.13 = (f32[2]{0:T(128)S(1)}, f32[32]{0:T(128)S(1)}, f32[2]{0:T(128)S(1)}) all-reduce(f32[2]{0:T(128)S(1)} %slice_dynamic-update-slice_fusion.1, f32[32]{0:T(128)S(1)} %get-tuple-element.98, f32[2]{0:T(128)S(1)} %get-tuple-element.70), channel_id=2, replica_groups=mesh['seq_0'=4,'seq_1'=4,'head_0'=4,'head_1'=2] {'head_1'}, use_global_device_ids=true, to_apply=%add | all-reduce | flops 36 | bytes 288
  20.7 1.3 dynamic-slice.2
  22.7 1.4 dynamic-update-slice.1
  24.0 1.4 dynamic-update-slice.6
  25.6 9.8 %all-reduce.10 = (f32[4]{0:T(128)S(1)}, f32[64]{0:T(128)S(1)}, f32[4]{0:T(128)S(1)}) all-reduce(f32[4]{0:T(128)S(1)} %dynamic-update-slice.1, f32[64]{0:T(128)S(1)} %get-tuple-element.96, f32[4]{0:T(128)S(1)} %dynamic-update-slice.6), channel_id=3, replica_groups=mesh['seq_0'=4,'seq_1'=4,'head_0'=4,'head_1'=2] {'head_0'}, use_global_device_ids=true, to_apply=%add.1 | all-reduce | flops 72 | bytes 576
  36.0 1.2 fusion.156
  37.3 1.3 dynamic-slice.3
  42.3 1.3 dynamic-update-slice.8
  43.6 1.4 dynamic-update-slice.2
  45.0 8.7 %all-reduce.11 = (f32[4]{0:T(128)S(1)}, f32[4]{0:T(128)S(1)}) all-reduce(f32[4]{0:T(128)S(1)} %dynamic-update-slice.2, f32[4]{0:T(128)S(1)} %dynamic-update-slice.8), channel_id=4, replica_groups=mesh['seq_0'=4,'seq_1'=4,'head_0'=4,'head_1'=2] {'seq_1'}, use_global_device_ids=true, to_apply=%add.2 | all-reduce | flops 8 | bytes 64
  54.3 1.3 fusion.157
  60.7 1.3 dynamic-update-slice.9
  62.0 1.3 dynamic-update-slice.3
  63.3 8.4 %all-reduce.12 = (f32[4]{0:T(128)S(1)}, f32[4]{0:T(128)S(1)}) all-reduce(f32[4]{0:T(128)S(1)} %dynamic-update-slice.3, f32[4]{0:T(128)S(1)} %dynamic-update-slice.9), channel_id=5, replica_groups=mesh['seq_0'=4,'seq_1'=4,'head_0'=4,'head_1'=2] {'seq_0'}, use_global_device_ids=true, to_apply=%add.3 | all-reduce | flops 8 | bytes 64
  80.2 3.9 %copy.27 = bf16[512,2048]{0,1:T(8,128)(2,1)} copy(bf16[512,2048]{1,0:T(8,128)(2,1)} %param.9) | data formatting | bytes 4194304 | tf_op jit(solution)/shard_map/while/body/jit(dynamic_index_in_dim)/squeeze | solution.py:81
  84.2 4.7 %fusion.31 = f32[16,128,128]{2,1,0:T(8,128)} fusion(bf16[512,16,128]{0,2,1:T(8,128)(2,1)} %bitcast.288, f32[512,16]{0,1:T(8,128)S(1)} %get-tuple-element.100, f32[16]{0:T(128)S(1)} %get-tuple-element.97, bf16[512,2048]{1,0:T(8,128)(2,1)} %param.10), kind=kOutput, calls=%fused_computation.35 | convolution fusion | flops 807665664 | bytes 5275712 | tf_op jit(solution)/shard_map/while/body/eval_jaxpr/jhd,jhe->hde/dot_general | solution.py:66
  88.9 14.2 %all-gather.27.cloned.1.call-done = f32[32,128,128]{2,1,0:T(8,128)} async-done(((f32[16,128,128]{2,1,0:T(8,128)}), f32[32,128,128]{2,1,0:T(8,128)}) %all-gather.27.cloned.1.call-update) | async-done | bytes 2097168 | tf_op jit(solution)/shard_map/all_gather | solution.py:26
  103.1 2.8 fusion.53
  119.8 35.7 %all-gather.19.cloned.1.call-done = f32[4,16,128,128]{3,2,1,0:T(8,128)} async-done(((f32[1,16,128,128]{3,2,1,0:T(8,128)}), f32[4,16,128,128]{3,2,1,0:T(8,128)}) %all-gather.19.cloned.1.call-update) | async-done | bytes 4194320 | tf_op jit(solution)/shard_map/all_gather | solution.py:26
  155.5 3.6 %multiply_add_fusion.1 = f32[1,16,128,128]{3,2,1,0:T(8,128)} fusion(f32[4,16,128,128]{3,2,1,0:T(8,128)} %all-gather.19.cloned.1.call-done, f32[16]{0:T(128)S(1)} %get-tuple-element.93, f32[16]{0:T(128)S(1)} %get-tuple-element.92, f32[16]{0:T(128)S(1)} %get-tuple-element.91, f32[16]{0:T(128)S(1)} %get-tuple-element.77), kind=kLoop, calls=%fused_computation.77 | loop fusion | flops 1835008 | bytes 5243136 | tf_op jit(solution)/shard_map/add | solution.py:103
  169.5 8.4 %all-gather.11 = f32[4,1,16]{2,1,0:T(1,128)S(1)} all-gather(f32[1,1,16]{2,1,0:T(1,128)S(1)} %get-tuple-element.76), channel_id=1, replica_groups=mesh['seq_0'=4,'seq_1'=4,'head_0'=4,'head_1'=2] {'seq_1'}, dimensions={0}, use_global_device_ids=true | all-gather | bytes 320 | tf_op jit(solution)/shard_map/all_gather | solution.py:26
  177.9 29.8 %all-gather.21.cloned.1.call-done = f32[4,16,128,128]{3,2,1,0:T(8,128)} async-done(((f32[1,16,128,128]{3,2,1,0:T(8,128)}), f32[4,16,128,128]{3,2,1,0:T(8,128)}) %all-gather.21.cloned.1.call-update) | async-done | bytes 4194320 | tf_op jit(solution)/shard_map/all_gather | solution.py:26
  207.7 3.6 %multiply_add_fusion = f32[1,16,128,128]{3,2,1,0:T(8,128)} fusion(f32[4,16,128,128]{3,2,1,0:T(8,128)} %all-gather.21.cloned.1.call-done, f32[16]{0:T(128)S(1)} %get-tuple-element.68, f32[16]{0:T(128)S(1)} %get-tuple-element.69, f32[16]{0:T(128)S(1)} %get-tuple-element.67, f32[16]{0:T(128)S(1)} %get-tuple-element.66), kind=kLoop, calls=%fused_computation.70 | loop fusion | flops 1835008 | bytes 5243136 | tf_op jit(solution)/shard_map/add | solution.py:103
  216.2 7.8 %all-gather.12 = f32[4,1,16]{2,1,0:T(1,128)S(1)} all-gather(f32[1,1,16]{2,1,0:T(1,128)S(1)} %bitcast.290), channel_id=1, replica_groups=mesh['seq_0'=4,'seq_1'=4,'head_0'=4,'head_1'=2] {'seq_0'}, dimensions={0}, use_global_device_ids=true | all-gather | bytes 320 | tf_op jit(solution)/shard_map/all_gather | solution.py:26
  224.5 3.3 fusion.18
  227.8 10.0 %fusion.13 = f32[16,512,128]{1,2,0:T(8,128)} fusion(bf16[512,16,128]{0,2,1:T(8,128)(2,1)} %bitcast.289, f32[512,512]{1,0:T(8,128)S(1)} %fusion.80, f32[16]{0:T(128)S(1)} %get-tuple-element.99, pred[512,512]{1,0:T(8,128)(4,1)S(1)} %fusion.82, bf16[512,2048]{1,0:T(8,128)(2,1)} %param.10, bf16[512,2048]{1,0:T(8,128)(2,1)S(1)} %copy-done), kind=kOutput, calls=%fused_computation.20 | convolution fusion | flops 2164260864 | bytes 11796544 | tf_op jit(solution)/shard_map/while/body/eval_jaxpr/hij,jhd->ihd/dot_general | solution.py:55
  237.9 22.2 %all-gather.23.cloned.1.call-done = f32[4,16,128,128]{3,2,1,0:T(8,128)} async-done(((f32[1,16,128,128]{3,2,1,0:T(8,128)}), f32[4,16,128,128]{3,2,1,0:T(8,128)}) %all-gather.23.cloned.1.call-update) | async-done | bytes 4194320 | tf_op jit(solution)/shard_map/all_gather | solution.py:26
  260.0 11.3 %fusion = (f32[512,16]{0,1:T(8,128)S(1)}, bf16[512,16,128]{0,2,1:T(8,128)(2,1)}) fusion(f32[4,16,128,128]{3,2,1,0:T(8,128)} %all-gather.23.cloned.1.call-done, f32[4,16,128,128]{3,2,1,0:T(8,128)} %all-gather.21.cloned.1.call-done, f32[4,16,128,128]{3,2,1,0:T(8,128)} %all-gather.19.cloned.1.call-done, f32[32,128,128]{2,1,0:T(8,128)} %all-gather.27.cloned.1.call-done, ...), kind=kOutput, calls=%fused_computation.5 | convolution fusion | flops 825221120 | bytes 27362382 | tf_op jit(solution)/shard_map/ihd,hde->ihe/dot_general | solution.py:92
  271.3 4.1 %convert_multiply_fusion.1 = f32[512,16,128]{0,2,1:T(8,128)} fusion(bf16[512,16,128]{0,2,1:T(8,128)(2,1)} %get-tuple-element.125, f32[512,16]{0,1:T(8,128)S(1)} %add_rsqrt_fusion), kind=kLoop, calls=%fused_computation.3 | loop fusion | flops 2097152 | bytes 6324224 | tf_op jit(solution)/shard_map/mul | solution.py:144
  275.4 5.4 %copy.24 = f32[512,2048]{1,0:T(8,128)} copy(f32[512,2048]{0,1:T(8,128)} %bitcast.287) | data formatting | bytes 8388608 | tf_op jit(solution)/shard_map/reshape | solution.py:144
  280.8 53.0 %all-gather.25.cloned.1.call-done = bf16[2048,2048]{1,0:T(8,128)(2,1)} async-done(((bf16[16,2048]{1,0:T(8,128)(2,1)}), bf16[2048,2048]{1,0:T(8,128)(2,1)}) %all-gather.25.cloned.1.call-update) | async-done | bytes 8388624 | tf_op jit(solution)/shard_map/all_gather | solution.py:148
  333.8 11.5 %convolution_convert_fusion = bf16[512,2048]{1,0:T(8,128)(2,1)} fusion(bf16[2048,2048]{1,0:T(8,128)(2,1)} %all-gather.25.cloned.1.call-done, bf16[512,2048]{1,0:T(8,128)(2,1)} %param.11, f32[512,2048]{1,0:T(8,128)} %copy.24, f32[2048]{0:T(1024)S(1)} %copy-done.1), kind=kOutput, calls=%fused_computation.19 | convolution fusion | flops 4304404480 | bytes 16785408 | tf_op jit(solution)/shard_map/dot_general | solution.py:146
  (53 shorter events, 15.5 us)
Async XLA Ops:
  6.5 218.0 %copy-start = (bf16[512,2048]{1,0:T(8,128)(2,1)S(1)}, bf16[512,2048]{1,0:T(8,128)(2,1)}, u32[]{:S(2)}) copy-start(bf16[512,2048]{1,0:T(8,128)(2,1)} %param.8) | copy-start | bytes 6291460
  6.5 96.6 %all-gather.27.cloned.1.call-start = ((), (), s32[]{:S(2)}) async-start(), calls=%async_computation.4 | async-start | bytes 3145728 | tf_op jit(solution)/shard_map/all_gather | solution.py:26
  88.8 66.6 %all-gather.19.cloned.1.call-start = ((), (), s32[]{:S(2)}) async-start(), calls=%async_computation | async-start | bytes 5242880 | tf_op jit(solution)/shard_map/all_gather | solution.py:26
  105.9 101.8 %all-gather.21.cloned.1.call-start = ((), (), s32[]{:S(2)}) async-start(), calls=%async_computation.1 | async-start | bytes 5242880 | tf_op jit(solution)/shard_map/all_gather | solution.py:26
  159.1 101.0 %all-gather.23.cloned.1.call-start = ((), (), s32[]{:S(2)}) async-start(), calls=%async_computation.2 | async-start | bytes 5242880 | tf_op jit(solution)/shard_map/all_gather | solution.py:26
  211.3 122.4 %all-gather.25.cloned.1.call-start = ((), (), s32[]{:S(2)}) async-start(), calls=%async_computation.3 | async-start | bytes 8454144 | tf_op jit(solution)/shard_map/all_gather | solution.py:148
  275.4 58.3 %copy-start.1 = (f32[2048]{0:T(1024)S(1)}, f32[2048]{0:T(1024)}, u32[]{:S(2)}) copy-start(f32[2048]{0:T(1024)} %param.14) | copy-start | bytes 24580
Sparse Core Ops, SparseCore 0:
  89.0 14.1 all-gather.26
  106.0 49.3 all-gather.18
  159.2 48.4 all-gather.20
  211.5 48.5 all-gather.22
  262.9 70.8 all-gather.24
where the time goes:
time: 353 us; the launch traced here: 352 us
  waiting for transfers between devices  155 us (44%)
  between operations  57.5 us (16%)
  blocking collectives  46.7 us (13%)
  matrix products  40.8 us (12%)
  local copies, waits for them, and re-layouts  25.8 us (7%)
  other arithmetic  25.5 us (7%)
    all_gather x4, waiting for transfers between devices, prefix_by_axis(): pieces = jax.tree.map(lambda part: lax.all_gather(part, axis), subtotal)  102 us
    all_gather x1, waiting for transfers between devices, on_device(): lax.all_gather(out_weight, SEQ_HEAD, axis=0, tiled=True)  53 us
    unnamed x4, blocking collectives  30.5 us
    all_gather x2, blocking collectives, prefix_by_axis(): pieces = jax.tree.map(lambda part: lax.all_gather(part, axis), subtotal)  16.2 us
    unnamed x26, local copies, waits for them, and re-layouts  15.2 us
    dot_general x1, matrix products, on_device(): jnp.dot(normed, lax.all_gather(out_weight, SEQ_HEAD, axis=0, tiled=True),...  11.5 us
    dot_general x1, matrix products, add_carried(): jnp.einsum('ihd,hde->ihe', queries.astype(jnp.float32), state_in, precisi...  11.3 us
    dot_general x1, matrix products, advance(): jnp.einsum('hij,jhd->ihd', weights, value_part, preferred_element_type=jn...  10 us
  transfers between devices with their start and end apart: 5, of which 5 were waited for; matrix products, arithmetic and copies ran while one was open for 10% of the time, Pallas kernels for 0%

commit v1 on v0

--- a/solution.py
+++ b/solution.py
@@ -145,7 +145,10 @@
     normed = (normed * norm_gain * jax.nn.silu(gate_rows.astype(jnp.float32))).astype(jnp.bfloat16)
     mixed_out = jnp.dot(
         normed,
-        lax.all_gather(out_weight, SEQ_HEAD, axis=0, tiled=True),
+        jnp.concatenate(
+            lax.all_to_all(jnp.stack([out_weight] * lax.axis_size(SEQ_HEAD)), SEQ_HEAD, 0, 0),
+            axis=0,
+        ),
         preferred_element_type=jnp.float32,
     )
     return mixed_out.astype(jnp.bfloat16)

time: 353 us -> 398 us (1.13)
  blocking collectives: 46.7 us -> 148 us
  waiting for transfers between devices: 155 us -> 84.4 us
  starting transfers between devices: 0.17 us -> 9.05 us
  local copies, waits for them, and re-layouts: 25.8 us -> 30.2 us
    all_gather x2, blocking collectives: 16.2 us -> 118 us  [prefix_by_axis(): pieces = jax.tree.map(lambda part: lax.all_gather(part, axis), subtotal)]
    all_gather x1 -> x0, waiting for transfers between devices: 53 us -> none  [on_device(): lax.all_gather(out_weight, SEQ_HEAD, axis=0, tiled=True)]
    all_gather x4, waiting for transfers between devices: 102 us -> 84.3 us  [prefix_by_axis(): pieces = jax.tree.map(lambda part: lax.all_gather(part, axis), subtotal)]
    all_to_all x0 -> x1, starting transfers between devices: none -> 8.93 us  [on_device(): lax.all_to_all(jnp.stack([out_weight] * lax.axis_size(SEQ_HEAD)), SEQ_HEA...]
    another operation x0 -> x1, local copies, waits for them, and re-layouts: none -> 4.29 us  [on_device(): jnp.stack([out_weight] * lax.axis_size(SEQ_HEAD))]
    unnamed x26 -> x30, local copies, waits for them, and re-layouts: 15.2 us -> 15.2 us
  transfers between devices with their start and end apart: 5 -> 5, of which waited for: 5 -> 4; matrix products, arithmetic and copies ran while one was open for 10% -> 11% of each run, Pallas kernels for 0% -> 0%
where the time goes in v1:
time: 398 us; the launch traced here: 396 us
  blocking collectives  148 us (37%)
  waiting for transfers between devices  84.4 us (21%)
  between operations  57.8 us (15%)
  matrix products  41.1 us (10%)
  local copies, waits for them, and re-layouts  30.2 us (8%)
  other arithmetic  25.6 us (6%)
  starting transfers between devices  9.05 us (2%)
    all_gather x2, blocking collectives, prefix_by_axis(): pieces = jax.tree.map(lambda part: lax.all_gather(part, axis), subtotal)  118 us
    all_gather x4, waiting for transfers between devices, prefix_by_axis(): pieces = jax.tree.map(lambda part: lax.all_gather(part, axis), subtotal)  84.3 us
    unnamed x4, blocking collectives  30.5 us
    unnamed x30, local copies, waits for them, and re-layouts  15.2 us
    dot_general x1, matrix products, on_device(): jnp.dot(normed, jnp.concatenate(lax.all_to_all(jnp.stack([out_weight] * l...  11.6 us
    dot_general x1, matrix products, add_carried(): jnp.einsum('ihd,hde->ihe', queries.astype(jnp.float32), state_in, precisi...  11.3 us
    dot_general x1, matrix products, advance(): jnp.einsum('hij,jhd->ihd', weights, value_part, preferred_element_type=jn...  10.3 us
    add x3, other arithmetic, link_pieces(): state_both = state_late + factor[:, None, None] * state_early  9.93 us
  transfers between devices with their start and end apart: 5, of which 4 were waited for; matrix products, arithmetic and copies ran while one was open for 11% of the time, Pallas kernels for 0%

profile of v1, /device:TPU:1, one launch (start us, length us, event | category | flops | bytes accessed | tf_op | source)
XLA Modules:
  0.0 396.3 jit_solution(13567369641189235093)
XLA Ops:
  10.2 1.3 slice_dynamic-update-slice_fusion
  14.3 3.5 all-reduce.13
  20.9 1.3 dynamic-slice.4
  22.2 1.3 dynamic-slice.3
  27.8 1.2 dynamic-update-slice.6
  29.2 9.8 %all-reduce.10 = (f32[4]{0:T(128)S(1)}, f32[64]{0:T(128)S(1)}, f32[4]{0:T(128)S(1)}) all-reduce(f32[4]{0:T(128)S(1)} %dynamic-update-slice.1, f32[64]{0:T(128)S(1)} %get-tuple-element.96, f32[4]{0:T(128)S(1)} %dynamic-update-slice.6), channel_id=3, replica_groups=mesh['seq_0'=4,'seq_1'=4,'head_0'=4,'head_1'=2] {'head_0'}, use_global_device_ids=true, to_apply=%add.1 | all-reduce | flops 72 | bytes 576
  45.3 1.4 dynamic-update-slice.2
  46.7 1.4 dynamic-update-slice.8
  48.1 8.7 %all-reduce.11 = (f32[4]{0:T(128)S(1)}, f32[4]{0:T(128)S(1)}) all-reduce(f32[4]{0:T(128)S(1)} %dynamic-update-slice.2, f32[4]{0:T(128)S(1)} %dynamic-update-slice.8), channel_id=4, replica_groups=mesh['seq_0'=4,'seq_1'=4,'head_0'=4,'head_1'=2] {'seq_1'}, use_global_device_ids=true, to_apply=%add.2 | all-reduce | flops 8 | bytes 64
  58.1 1.3 fusion.157
  63.1 1.4 dynamic-update-slice.3
  64.5 1.3 dynamic-update-slice.9
  65.7 8.4 %all-reduce.12 = (f32[4]{0:T(128)S(1)}, f32[4]{0:T(128)S(1)}) all-reduce(f32[4]{0:T(128)S(1)} %dynamic-update-slice.3, f32[4]{0:T(128)S(1)} %dynamic-update-slice.9), channel_id=5, replica_groups=mesh['seq_0'=4,'seq_1'=4,'head_0'=4,'head_1'=2] {'seq_0'}, use_global_device_ids=true, to_apply=%add.3 | all-reduce | flops 8 | bytes 64
  80.8 3.9 copy.27
  84.8 4.7 %fusion.31 = f32[16,128,128]{2,1,0:T(8,128)} fusion(bf16[512,16,128]{0,2,1:T(8,128)(2,1)} %bitcast.289, f32[512,16]{0,1:T(8,128)S(1)} %get-tuple-element.100, f32[16]{0:T(128)S(1)} %get-tuple-element.97, bf16[512,2048]{1,0:T(8,128)(2,1)} %param.10), kind=kOutput, calls=%fused_computation.35 | convolution fusion | flops 807665664 | bytes 5275712 | tf_op jit(solution)/shard_map/while/body/eval_jaxpr/jhd,jhe->hde/dot_general | solution.py:66
  89.5 14.2 %all-gather.24.cloned.1.call-done = f32[32,128,128]{2,1,0:T(8,128)} async-done(((f32[16,128,128]{2,1,0:T(8,128)}), f32[32,128,128]{2,1,0:T(8,128)}) %all-gather.24.cloned.1.call-update) | async-done | bytes 2097168 | tf_op jit(solution)/shard_map/all_gather | solution.py:26
  103.8 2.7 fusion.53
  120.6 35.5 %all-gather.18.cloned.1.call-done = f32[4,16,128,128]{3,2,1,0:T(8,128)} async-done(((f32[1,16,128,128]{3,2,1,0:T(8,128)}), f32[4,16,128,128]{3,2,1,0:T(8,128)}) %all-gather.18.cloned.1.call-update) | async-done | bytes 4194320 | tf_op jit(solution)/shard_map/all_gather | solution.py:26
  156.1 3.6 multiply_add_fusion.1
  159.7 4.3 %stack.2 = bf16[128,16,2048]{2,1,0:T(8,128)(2,1)} broadcast(bf16[16,2048]{1,0:T(8,128)(2,1)S(1)} %copy-done.2), dimensions={1,2} | broadcast | bytes 8454144 | tf_op jit(solution)/shard_map/stack | solution.py:149
  164.0 8.9 %all-to-all-start = ((bf16[128,16,2048]{2,1,0:T(8,128)(2,1)}), bf16[128,16,2048]{2,1,0:T(8,128)(2,1)}, u32[]{:S(2)}, u32[]{:S(2)}) async-start(bf16[128,16,2048]{2,1,0:T(8,128)(2,1)} %stack.2), calls=%async_computation | async-start | bytes 16777216 | tf_op jit(solution)/shard_map/all_to_all | solution.py:149
  183.0 108.2 %all-gather.11 = f32[4,1,16]{2,1,0:T(1,128)S(1)} all-gather(f32[1,1,16]{2,1,0:T(1,128)S(1)} %get-tuple-element.76), channel_id=1, replica_groups=mesh['seq_0'=4,'seq_1'=4,'head_0'=4,'head_1'=2] {'seq_1'}, dimensions={0}, use_global_device_ids=true | all-gather | bytes 320 | tf_op jit(solution)/shard_map/all_gather | solution.py:26
  291.2 8.5 %all-gather.20.cloned.1.call-done = f32[4,16,128,128]{3,2,1,0:T(8,128)} async-done(((f32[1,16,128,128]{3,2,1,0:T(8,128)}), f32[4,16,128,128]{3,2,1,0:T(8,128)}) %all-gather.20.cloned.1.call-update) | async-done | bytes 4194320 | tf_op jit(solution)/shard_map/all_gather | solution.py:26
  299.7 3.6 multiply_add_fusion
  307.5 9.6 %all-gather.12 = f32[4,1,16]{2,1,0:T(1,128)S(1)} all-gather(f32[1,1,16]{2,1,0:T(1,128)S(1)} %bitcast.291), channel_id=1, replica_groups=mesh['seq_0'=4,'seq_1'=4,'head_0'=4,'head_1'=2] {'seq_0'}, dimensions={0}, use_global_device_ids=true | all-gather | bytes 320 | tf_op jit(solution)/shard_map/all_gather | solution.py:26
  317.7 3.3 fusion.18
  320.9 10.3 %fusion.13 = f32[16,512,128]{1,2,0:T(8,128)} fusion(bf16[512,16,128]{0,2,1:T(8,128)(2,1)} %bitcast.290, f32[512,512]{1,0:T(8,128)S(1)} %fusion.80, f32[16]{0:T(128)S(1)} %get-tuple-element.99, pred[512,512]{1,0:T(8,128)(4,1)S(1)} %fusion.82, bf16[512,2048]{1,0:T(8,128)(2,1)} %param.10, bf16[512,2048]{1,0:T(8,128)(2,1)S(1)} %copy-done), kind=kOutput, calls=%fused_computation.20 | convolution fusion | flops 2164260864 | bytes 11796544 | tf_op jit(solution)/shard_map/while/body/eval_jaxpr/hij,jhd->ihd/dot_general | solution.py:55
  331.2 26.1 %all-gather.22.cloned.1.call-done = f32[4,16,128,128]{3,2,1,0:T(8,128)} async-done(((f32[1,16,128,128]{3,2,1,0:T(8,128)}), f32[4,16,128,128]{3,2,1,0:T(8,128)}) %all-gather.22.cloned.1.call-update) | async-done | bytes 4194320 | tf_op jit(solution)/shard_map/all_gather | solution.py:26
  357.3 11.3 %fusion = (f32[512,16]{0,1:T(8,128)S(1)}, bf16[512,16,128]{0,2,1:T(8,128)(2,1)}) fusion(f32[4,16,128,128]{3,2,1,0:T(8,128)} %all-gather.22.cloned.1.call-done, f32[4,16,128,128]{3,2,1,0:T(8,128)} %all-gather.20.cloned.1.call-done, f32[4,16,128,128]{3,2,1,0:T(8,128)} %all-gather.18.cloned.1.call-done, f32[32,128,128]{2,1,0:T(8,128)} %all-gather.24.cloned.1.call-done, ...), kind=kOutput, calls=%fused_computation.5 | convolution fusion | flops 825221120 | bytes 27362382 | tf_op jit(solution)/shard_map/ihd,hde->ihe/dot_general | solution.py:92
  368.6 4.2 %convert_multiply_fusion.1 = f32[512,16,128]{0,2,1:T(8,128)} fusion(bf16[512,16,128]{0,2,1:T(8,128)(2,1)} %get-tuple-element.125, f32[512,16]{0,1:T(8,128)S(1)} %add_rsqrt_fusion), kind=kLoop, calls=%fused_computation.3 | loop fusion | flops 2097152 | bytes 6324224 | tf_op jit(solution)/shard_map/mul | solution.py:144
  372.8 5.4 %copy.24 = f32[512,2048]{1,0:T(8,128)} copy(f32[512,2048]{0,1:T(8,128)} %bitcast.288) | data formatting | bytes 8388608 | tf_op jit(solution)/shard_map/reshape | solution.py:144
  378.2 11.6 %convolution_convert_fusion = bf16[512,2048]{1,0:T(8,128)(2,1)} fusion(bf16[2048,2048]{1,0:T(8,128)(2,1)} %bitcast.77, bf16[512,2048]{1,0:T(8,128)(2,1)} %param.11, f32[512,2048]{1,0:T(8,128)} %copy.24, f32[2048]{0:T(1024)S(1)} %copy-done.3), kind=kOutput, calls=%fused_computation.19 | convolution fusion | flops 4304404480 | bytes 16785408 | tf_op jit(solution)/shard_map/dot_general | solution.py:146
  (57 shorter events, 16.3 us)
Async XLA Ops:
  6.5 311.1 %copy-start = (bf16[512,2048]{1,0:T(8,128)(2,1)S(1)}, bf16[512,2048]{1,0:T(8,128)(2,1)}, u32[]{:S(2)}) copy-start(bf16[512,2048]{1,0:T(8,128)(2,1)} %param.8) | copy-start | bytes 6291460
  6.5 97.2 %all-gather.24.cloned.1.call-start = ((), (), s32[]{:S(2)}) async-start(), calls=%async_computation.4 | async-start | bytes 3145728 | tf_op jit(solution)/shard_map/all_gather | solution.py:26
  89.5 66.6 %all-gather.18.cloned.1.call-start = ((), (), s32[]{:S(2)}) async-start(), calls=%async_computation.1 | async-start | bytes 5242880 | tf_op jit(solution)/shard_map/all_gather | solution.py:26
  106.5 53.2 %copy-start.2 = (bf16[16,2048]{1,0:T(8,128)(2,1)S(1)}, bf16[16,2048]{1,0:T(8,128)(2,1)}, u32[]{:S(2)}) copy-start(bf16[16,2048]{1,0:T(8,128)(2,1)} %param.15) | copy-start | bytes 196612
  106.5 193.1 %all-gather.20.cloned.1.call-start = ((), (), s32[]{:S(2)}) async-start(), calls=%async_computation.2 | async-start | bytes 5242880 | tf_op jit(solution)/shard_map/all_gather | solution.py:26
  164.0 214.1 %all-to-all-start = ((bf16[128,16,2048]{2,1,0:T(8,128)(2,1)}), bf16[128,16,2048]{2,1,0:T(8,128)(2,1)}, u32[]{:S(2)}, u32[]{:S(2)}) async-start(bf16[128,16,2048]{2,1,0:T(8,128)(2,1)} %stack.2), calls=%async_computation | async-start | bytes 16777216 | tf_op jit(solution)/shard_map/all_to_all | solution.py:149
  173.0 184.3 %all-gather.22.cloned.1.call-start = ((), (), s32[]{:S(2)}) async-start(), calls=%async_computation.3 | async-start | bytes 5242880 | tf_op jit(solution)/shard_map/all_gather | solution.py:26
  372.8 5.4 %copy-start.3 = (f32[2048]{0:T(1024)S(1)}, f32[2048]{0:T(1024)}, u32[]{:S(2)}) copy-start(f32[2048]{0:T(1024)} %param.14) | copy-start | bytes 24580
  378.2 11.6 %copy-start.1 = (bf16[512,2048]{1,0:T(8,128)(2,1)S(1)}, bf16[512,2048]{1,0:T(8,128)(2,1)}, u32[]{:S(2)}) copy-start(bf16[512,2048]{1,0:T(8,128)(2,1)} %param.8) | copy-start | bytes 6291460
Sparse Core Ops, SparseCore 0:
  89.6 14.1 all-gather.23
  106.7 49.3 all-gather.17
  159.8 139.7 all-gather.19
  303.4 53.8 all-gather.21
